TPU v7x, 256 devices: a whole 4x4x8 slice. The times are simulated.
256 devices in a mesh: group: 4 (over z_hi), member: 64 (over y, x, z_lo, core).
Axes of the slice: x: 4, y: 4, z: 8 (z_hi: 4, z_lo: 2; z = z_hi * 2 + z_lo), core: 2. Of those that a mesh axis runs over, the one named last changes fastest.
Arguments:
- audio_vectors: bfloat16 [32768, 768], P(('group', 'member')), may hold values from -8 to 8
- sentence_vectors: bfloat16 [16384, 768], P(('group', 'member')), may hold values from -8 to 8
- matching_indices: int32 [32768], P(('group', 'member')), may hold values from 0 to 16383, as said below
- sharpness_array: float32 [1], replicated, may hold values from 8 to 16
- offset_term: float32 [1], replicated, may hold values from -4 to -2
Outputs:
- speech_grad: float32 [32768, 768], P(('group', 'member'))
- text_grad: float32 [16384, 768], P(('group', 'member'))
Inputs may be any that keep to these rules, and one draw needn't show every extreme that they name: `matching_indices`: each caption matches exactly two speech clips.
All inputs are finite; a program needn't handle non-finite values.
Results may differ from a plain program's by a relative error of at most 0.00072.
Values may be sent and summed in bfloat16 or wider, within the bound.
A program may use at most 128 MiB of HBM per device.

v0:
```python
import jax
import jax.numpy as jnp
from jax import lax
from jax.sharding import Mesh
from jax.sharding import PartitionSpec as P

MEMBER = ("member_0", "member_1", "member_2", "member_3")
GROUP_MEMBER = ("group", "member_0", "member_1", "member_2", "member_3")


def joined_along(blocks, dim):
    blocks = jnp.moveaxis(blocks, 0, dim)
    lengths = blocks.shape
    return blocks.reshape(*lengths[:dim], lengths[dim] * lengths[dim + 1], *lengths[dim + 2 :])


def copy_for_each(value, axis):
    size = lax.axis_size(axis)
    return lax.all_to_all(
        jnp.broadcast_to(value[None], (size, *value.shape)), axis, 0, 0, tiled=True
    )


def gather_directly(value, axis, dim):
    return joined_along(copy_for_each(value, axis), dim)


def split_up(value, dim, size):
    before, after = (value.shape[:dim], value.shape[dim + 1 :])
    return jnp.moveaxis(value.reshape(*before, size, -1, *after), dim, 0)


def sum_at_owner(value, axis, dim):
    size = lax.axis_size(axis)
    blocks = lax.all_to_all(split_up(value, dim, size), axis, 0, 0, tiled=True)
    return jnp.sum(blocks, axis=0)


def scatter_pairs(value, chips, core, dim):
    sizes = (lax.axis_size(chips), lax.axis_size(core))
    blocks = split_up(value, dim, sizes[0] * sizes[1])
    inside = blocks.shape[1:]
    blocks = blocks.reshape(*sizes, *inside).swapaxes(0, 1).reshape(-1, *inside)
    blocks = lax.psum_scatter(blocks, core, scatter_dimension=0, tiled=True)
    return lax.psum_scatter(blocks, chips, scatter_dimension=0, tiled=True)[0]


def unit_rows(values):
    floats = values.astype(jnp.float32)
    norms = jnp.sqrt(jnp.sum(floats * floats, axis=-1, keepdims=True) + 1e-06)
    return (floats / norms, norms)


def project_gradient(back, direction, norms):
    along = jnp.sum(direction * back, axis=-1, keepdims=True)
    return (back - direction * along) / norms


def pair_coef(audio_entries, label_rows, text_rows, columns, sharpness_factor, shift):
    logits = (
        sharpness_factor * jnp.dot(audio_entries, text_rows.T, preferred_element_type=jnp.float32)
        + shift
    )
    match = (label_rows[:, None] == columns[None, :]).astype(jnp.float32)
    return (sharpness_factor * (jax.nn.sigmoid(logits) - match)).astype(jnp.bfloat16)


def column_product(pair_weight, visitor):
    return lax.dot_general(
        pair_weight, visitor, (((0,), (0,)), ((), ())), preferred_element_type=jnp.float32
    )


def shards(audio_vectors, sentence_vectors, matching_indices, sharpness_array, offset_term):
    audio_heading, speech_norm = unit_rows(audio_vectors)
    text_dir, text_norm = unit_rows(sentence_vectors)
    speech_unit = audio_heading.astype(jnp.bfloat16)
    text_normalized = text_dir.astype(jnp.bfloat16)
    sharpness_factor = sharpness_array[0]
    shift = offset_term[0]
    group_now = lax.axis_index("group")
    text_rows = lax.all_gather(text_normalized, MEMBER, axis=0, tiled=True)
    width = text_rows.shape[0]
    columns = group_now * width + jnp.arange(width, dtype=jnp.int32)
    label_all = lax.all_gather(matching_indices, "group", axis=0, tiled=True)
    speech_all = gather_directly(speech_unit, "group", 0)
    pair_weight = pair_coef(speech_all, label_all, text_rows, columns, sharpness_factor, shift)
    speech_part = jnp.dot(pair_weight, text_rows, preferred_element_type=jnp.float32)
    speech_gradient_back = sum_at_owner(speech_part, "group", 0)
    text_part = column_product(pair_weight, speech_all)
    text_back = scatter_pairs(text_part, ("member_0", "member_1", "member_2"), "member_3", 0)
    speech_grad = project_gradient(speech_gradient_back, audio_heading, speech_norm)
    text_grad = project_gradient(text_back, text_dir, text_norm)
    return (speech_grad, text_grad)


def solution(mesh):
    split = Mesh(
        mesh.devices.reshape(mesh.shape["group"], 4, 4, 2, 2),
        ("group", "member_0", "member_1", "member_2", "member_3"),
    )
    return jax.shard_map(
        shards,
        mesh=split,
        in_specs=(P(GROUP_MEMBER, None), P(GROUP_MEMBER, None), P(GROUP_MEMBER), P(), P()),
        out_specs=(P(GROUP_MEMBER, None), P(GROUP_MEMBER, None)),
        check_vma=False,
    )
```

profile of v0, /device:TPU:64, one launch (start us, length us, event | category | flops | bytes accessed | tf_op | source)
XLA Modules:
  0.0 414.7 jit_solution(13824116031976714388)
XLA Ops:
  7.2 0.0 all-gather.3.cloned.1.call-start
  7.2 1.0 fusion.7
  8.2 1.6 fusion.10
  9.9 0.0 all-gather.3.cloned.1.call-update
  9.9 1.0 fusion.6
  11.0 1.0 fusion.11
  12.0 0.9 broadcast_in_dim.2
  12.9 8.1 %all-to-all-start = ((bf16[4,128,768]{2,1,0:T(8,128)(2,1)}), bf16[4,128,768]{2,1,0:T(8,128)(2,1)S(1)}, u32[]{:S(2)}, u32[]{:S(2)}) async-start(bf16[4,128,768]{2,1,0:T(8,128)(2,1)} %broadcast_in_dim.2), calls=%async_computation | async-start | bytes 1572864 | tf_op jit(solution)/shard_map/all_to_all | solution.py:19
  21.0 0.0 reduce-scatter.3.cloned.1.call-start
  22.3 27.0 %all-gather = s32[4,1,128]{2,1,0:T(1,128)S(1)} all-gather(s32[1,1,128]{2,1,0:T(1,128)} %bitcast.42), channel_id=1, replica_groups=mesh['group'=4,'member_0'=4,'member_1'=4,'member_2'=2,'member_3'=2] {'gr..., dimensions={0}, use_global_device_ids=true | all-gather | bytes 2560 | tf_op jit(solution)/shard_map/all_gather | solution.py:85
  49.4 0.0 all-to-all-done
  49.4 75.7 %all-gather.3.cloned.1.call-done = bf16[4096,768]{1,0:T(8,128)(2,1)} async-done(((bf16[64,768]{1,0:T(8,128)(2,1)}), bf16[4096,768]{1,0:T(8,128)(2,1)}) %all-gather.3.cloned.1.call-update) | async-done | bytes 6291472 | tf_op jit(solution)/shard_map/all_gather | solution.py:82
  125.0 10.1 %fusion.1 = (bf16[4096,512]{0,1:T(8,128)(2,1)}, f32[512,4096]{1,0:T(8,128)}) fusion(s32[4096]{0:T(1024)S(1)} %iota_add_fusion, f32[]{:T(128)} %bitcast.33, s32[512]{0:T(512)S(1)} %bitcast.40, f32[]{:T(128)} %bitcast.34, bf16[512,768]{1,0:T(8,128)(2,1)S(1)} %bitcast.38, bf16[4096,768]{1,0:T(8,128)(2,1)} %all-gather.3.cloned.1.call-done), kind=kOutput, calls=%fused_computation.2 | convolution fusion | flops 3242196992 | bytes 19679240 | tf_op jit(solution)/shard_map/dot_general | solution.py:61
  135.2 6.5 %copy.10 = bf16[4096,512]{1,0:T(8,128)(2,1)} copy(bf16[4096,512]{0,1:T(8,128)(2,1)} %get-tuple-element.2) | data formatting | bytes 8388608 | tf_op jit(solution)/shard_map/convert_element_type | solution.py:65
  141.7 10.2 %convolution_bitcast_fusion = f32[2,32,64,768]{3,2,0,1:T(8,128)} fusion(bf16[32,2,64,512]{3,2,1,0:T(8,128)(2,1)} %bitcast.36, bf16[512,768,1,1]{1,0,3,2:T(8,128)(2,1)S(1)} %bitcast.39), kind=kOutput, calls=%fused_computation.5 | convolution fusion | flops 3221225472 | bytes 17563648 | tf_op jit(solution)/shard_map/dot_general | solution.py:69
  151.9 10.5 %copy.11 = f32[2,32,64,768]{3,2,1,0:T(8,128)} copy(f32[2,32,64,768]{3,2,0,1:T(8,128)} %convolution_bitcast_fusion) | data formatting | bytes 25165824 | tf_op jit(solution)/shard_map/transpose | solution.py:43
  162.4 0.0 reduce-scatter.3.cloned.1.call-update
  162.4 0.0 reduce-scatter.5.cloned.1.call-start
  162.5 27.0 %reduce-scatter.3.cloned.1.call-done = f32[32,64,768]{2,1,0:T(8,128)} async-done(((f32[64,64,768]{2,1,0:T(8,128)}), f32[32,64,768]{2,1,0:T(8,128)}) %reduce-scatter.3.cloned.1.call-update) | async-done | bytes 6291472 | tf_op jit(solution)/shard_map/reduce_scatter | solution.py:44
  189.4 0.0 reduce-scatter.5.cloned.1.call-update
  189.5 0.0 copy-start
  189.5 0.0 copy-start.1
  189.5 8.0 %fusion.2 = f32[512,768]{1,0:T(8,128)S(1)} fusion(bf16[4096,768]{1,0:T(8,128)(2,1)} %all-gather.3.cloned.1.call-done, f32[512,4096]{1,0:T(8,128)} %get-tuple-element.3, s32[4096]{0:T(1024)S(1)} %iota_add_fusion, f32[]{:T(128)} %bitcast.32, s32[512]{0:T(512)S(1)} %bitcast.41), kind=kOutput, calls=%fused_computation.6 | convolution fusion | flops 3231711232 | bytes 16271364 | tf_op jit(solution)/shard_map/dot_general | solution.py:88
  197.5 60.5 %all_to_all.10 = f32[4,128,768]{2,1,0:T(8,128)S(1)} all-to-all(f32[4,128,768]{2,1,0:T(8,128)S(1)} %bitcast.37), channel_id=1, replica_groups=mesh['group'=4,'member_0'=4,'member_1'=4,'member_2'=2,'member_3'=2] {'gr..., dimensions={0} | all-to-all | bytes 3145728 | tf_op jit(solution)/shard_map/all_to_all | solution.py:35
  258.0 0.1 reduce_sum.47
  258.1 0.0 copy-done
  258.1 0.2 multiply_reduce_fusion
  258.3 0.9 subtract_divide_fusion
  259.2 146.1 %reduce-scatter.5.cloned.1.call-done = f32[1,64,768]{2,1,0:T(8,128)} async-done(((f32[32,64,768]{2,1,0:T(8,128)}), f32[1,64,768]{2,1,0:T(8,128)}) %reduce-scatter.5.cloned.1.call-update) | async-done | bytes 196624 | tf_op jit(solution)/shard_map/reduce_scatter | solution.py:45
  405.4 0.0 copy-done.1
  405.4 1.1 fusion.8
  406.5 1.7 fusion.9
  (3 shorter events, 0.0 us)
Async XLA Ops:
  7.2 117.9 %all-gather.3.cloned.1.call-start = ((), (), s32[]{:S(2)}) async-start(), calls=%async_computation.4 | async-start | bytes 6389760 | tf_op jit(solution)/shard_map/all_gather | solution.py:82
  12.9 36.4 %all-to-all-start = ((bf16[4,128,768]{2,1,0:T(8,128)(2,1)}), bf16[4,128,768]{2,1,0:T(8,128)(2,1)S(1)}, u32[]{:S(2)}, u32[]{:S(2)}) async-start(bf16[4,128,768]{2,1,0:T(8,128)(2,1)} %broadcast_in_dim.2), calls=%async_computation | async-start | bytes 1572864 | tf_op jit(solution)/shard_map/all_to_all | solution.py:19
  21.0 168.4 %reduce-scatter.3.cloned.1.call-start = ((), (), s32[]{:S(2)}) async-start(), calls=%async_computation.5 | async-start | bytes 18874368 | tf_op jit(solution)/shard_map/reduce_scatter | solution.py:44
  162.4 242.9 %reduce-scatter.5.cloned.1.call-start = ((), (), s32[]{:S(2)}) async-start(), calls=%async_computation.6 | async-start | bytes 6488064 | tf_op jit(solution)/shard_map/reduce_scatter | solution.py:45
  189.5 68.7 %copy-start = (bf16[128,768]{1,0:T(8,128)(2,1)S(1)}, bf16[128,768]{1,0:T(8,128)(2,1)}, u32[]{:S(2)}) copy-start(bf16[128,768]{1,0:T(8,128)(2,1)} %param.5) | copy-start | bytes 589828
  189.5 215.9 %copy-start.1 = (bf16[64,768]{1,0:T(8,128)(2,1)S(1)}, bf16[64,768]{1,0:T(8,128)(2,1)}, u32[]{:S(2)}) copy-start(bf16[64,768]{1,0:T(8,128)(2,1)} %param.6) | copy-start | bytes 294916
Sparse Core Ops, SparseCore 0:
  10.4 114.5 all-gather.2
  162.5 26.8 reduce-scatter.2
  192.0 213.3 reduce-scatter.4
where the time goes:
time: 415 us
  waiting for transfers between devices  249 us (60%)
  blocking collectives  87.5 us (21%)
  matrix products  28.3 us (7%)
  local copies, waits for them, and re-layouts  18 us (4%)
  between operations  15.1 us (4%)
  other arithmetic  8.8 us (2%)
  starting transfers between devices  8.19 us (2%)
    reduce_scatter x1, waiting for transfers between devices, scatter_pairs(): return lax.psum_scatter(blocks, chips, scatter_dimension=0, tiled=True)[0]  146 us
    all_gather x1, waiting for transfers between devices, shards(): text_rows = lax.all_gather(text_normalized, MEMBER, axis=0, tiled=True)  75.7 us
    all_to_all x1, blocking collectives, sum_at_owner(): blocks = lax.all_to_all(split_up(value, dim, size), axis, 0, 0, tiled=True)  60.5 us
    all_gather x1, blocking collectives, shards(): label_all = lax.all_gather(matching_indices, 'group', axis=0, tiled=True)  27 us
    reduce_scatter x1, waiting for transfers between devices, scatter_pairs(): blocks = lax.psum_scatter(blocks, core, scatter_dimension=0, tiled=True)  27 us
    transpose x1, local copies, waits for them, and re-layouts, scatter_pairs(): blocks = blocks.reshape(*sizes, *inside).swapaxes(0, 1).reshape(-1, *inside)  10.5 us
    dot_general x1, matrix products, column_product(): lax.dot_general(pair_weight, visitor, (((0,), (0,)), ((), ())), preferred...  10.2 us
    dot_general x1, matrix products, pair_coef(): jnp.dot(audio_entries, text_rows.T, preferred_element_type=jnp.float32)  10.1 us
  transfers between devices with their start and end apart: 4, of which 3 were waited for; matrix products, arithmetic and copies ran while one was open for 3% of the time, Pallas kernels for 0%

commit v1 on v0

v1 whole, which is shorter than its diff:
```python
import functools

import jax
import jax.numpy as jnp
from jax import lax
from jax.experimental import pallas as pl
from jax.experimental.pallas import tpu as pltpu
from jax.sharding import Mesh
from jax.sharding import PartitionSpec as P

AXES = ("zh", "y", "x", "zl", "c")
MESH_ID = pl.DeviceIdType.MESH
F32 = jnp.float32
BF16 = jnp.bfloat16

L1, R1, L2, R2, L3, R3, OWN, D4 = range(8)
NR, NT, E = 128, 64, 768
HALF = NR // 2
SLAB = 128
SUB = 32
CHUNK = 512


def unit(values):
    floats = values.astype(F32)
    norms = jnp.sqrt(jnp.sum(floats * floats, axis=-1, keepdims=True) + 1e-06)
    return floats / norms, norms


def project(back, values):
    direction, norms = unit(values)
    along = jnp.sum(direction * back, axis=-1, keepdims=True)
    return (back - direction * along) / norms


def kernel(
    sharp_ref, shift_ref, audio_ref, text_ref, label_ref,
    speech_out, text_out,
    s_all, t_all, labels, ids, t_back, s_back,
    z_from_left, z_from_right, sib_back, slab_low, slab_high, sub_low, sub_high,
    send_sems, recv_sems,
):
    zh, y, x, zl, c = (lax.axis_index(a) for a in AXES)
    z = zh * 2 + zl

    def at_z(step):
        other = (z + step) % 8
        return (other // 2, y, x, other % 2, c)

    def at_y(step):
        return (zh, (y + step) % 4, x, zl, c)

    def at_x(step):
        return (zh, y, (x + step) % 4, zl, c)

    sibling = (zh, y, x, zl, 1 - c)
    copies = {}

    def copy(name, src, dst, device):
        q = len(copies)
        copies[name] = pltpu.make_async_remote_copy(
            src_ref=src, dst_ref=dst, send_sem=send_sems.at[q], recv_sem=recv_sems.at[q],
            device_id=device, device_id_type=MESH_ID,
        )

    def start(*names):
        for name in names:
            copies[name].start()

    def wait(*names):
        for name in names:
            copies[name].wait_recv()

    def s_rows(slot, half=None):
        if half is None:
            return s_all.at[pl.ds(slot * NR, NR)]
        return s_all.at[pl.ds(slot * NR + half * HALF, HALF)]

    def t_base(k, core, which):
        return k * CHUNK + core * 2 * SLAB + which * SLAB

    def t_rows(k, core, which, first, count):
        return t_all.at[pl.ds(t_base(k, core, which) + first, count)]

    def lab(slot):
        return labels.at[pl.ds(slot * 8, 8)]

    up = ((OWN, L1), (L1, L2), (L2, L3))
    down = ((OWN, R1), (R1, R2), (R2, R3))
    for pairs, step in ((up, 1), (down, -1)):
        for src, dst in pairs:
            for half in (0, 1):
                copy(("s", dst, half), s_rows(src, half), s_rows(dst, half), at_z(step))
            copy(("l", dst), lab(src), lab(dst), at_z(step))
    copy(("s", D4, 0), s_rows(L3, 0), s_rows(D4, 0), at_z(1))
    copy(("s", D4, 1), s_rows(R3, 1), s_rows(D4, 1), at_z(-1))
    copy(("l", D4), lab(L3), lab(D4), at_z(1))

    for w, (first, second) in enumerate(((at_x, at_y), (at_y, at_x))):
        piece = lambda j, lo=0, n=SUB: t_rows(0, 0, w, j * SUB + lo, n)
        copy(("t1", w, 1), piece(0), piece(1), first(1))
        copy(("t1", w, 2), piece(0), piece(2), first(-1))
        copy(("t1", w, 3, 0), piece(1, 0, 16), piece(3, 0, 16), first(1))
        copy(("t1", w, 3, 1), piece(2, 16, 16), piece(3, 16, 16), first(-1))
        for j in range(4):
            copy(("t2", w, 1, j), piece(j), t_rows(1, 0, w, j * SUB, SUB), second(1))
            copy(("t2", w, 2, j), piece(j), t_rows(2, 0, w, j * SUB, SUB), second(-1))
        copy(("t2", w, 3, 0), t_rows(1, 0, w, 0, 64), t_rows(3, 0, w, 0, 64), second(1))
        copy(("t2", w, 3, 1), t_rows(2, 0, w, 64, 64), t_rows(3, 0, w, 64, 64), second(-1))
        for k in range(4):
            copy(("ts", w, k), t_rows(k, 0, w, 0, SLAB), t_rows(k, 1, w, 0, SLAB), sibling)

    def sb(slot, half):
        return s_back.at[pl.ds(slot * NR + half * HALF, HALF)]

    def landing(buf, order, half):
        return buf.at[pl.ds((order * 2 + half) * HALF, HALF)]

    for buf, chain, step, d4half in (
        (z_from_left, (D4, R3, R2, R1, OWN), 1, 0), (z_from_right, (D4, L3, L2, L1, OWN), -1, 1)
    ):
        for order, src in enumerate(chain[:-1]):
            for half in (0, 1):
                if src == D4 and half != d4half:
                    continue
                copy(("zr", step, order, half), sb(src, half), landing(buf, order, half), at_z(step))

    def tb(k, which, first, count):
        return t_back.at[pl.ds(t_base(k, 0, which) + first, count)]

    for k in range(4):
        copy(
            ("sr", k), t_back.at[pl.ds(t_base(k, 1, 0), 2 * SLAB)],
            sib_back.at[pl.ds(k * 2 * SLAB, 2 * SLAB)], sibling,
        )
    for w, (first, second) in enumerate(((at_x, at_y), (at_y, at_x))):
        slab_at = lambda buf, order, half: buf.at[pl.ds(w * 256 + order * 128 + half * 64, 64)]
        sub_at = lambda buf, order, half: buf.at[pl.ds(w * 64 + order * 32 + half * 16, 16)]
        for buf, k, step, d2half in ((slab_low, 2, 1, 0), (slab_high, 1, -1, 1)):
            copy(("r2", w, step, 0, d2half), tb(3, w, d2half * 64, 64), slab_at(buf, 0, d2half), second(step))
            for half in (0, 1):
                copy(("r2", w, step, 1, half), tb(k, w, half * 64, 64), slab_at(buf, 1, half), second(step))
        for buf, j, step, d2half in ((sub_low, 2, 1, 0), (sub_high, 1, -1, 1)):
            copy(
                ("r1", w, step, 0, d2half), tb(0, w, 3 * SUB + d2half * 16, 16),
                sub_at(buf, 0, d2half), first(step),
            )
            for half in (0, 1):
                copy(
                    ("r1", w, step, 1, half), tb(0, w, j * SUB + half * 16, 16),
                    sub_at(buf, 1, half), first(step),
                )

    barrier = pltpu.get_barrier_semaphore()
    for device in (at_z(1), at_z(-1), at_y(1), at_y(-1), at_x(1), at_x(-1), sibling):
        pl.semaphore_signal(barrier, inc=1, device_id=device, device_id_type=MESH_ID)

    s_all[pl.ds(OWN * NR, NR), :] = unit(audio_ref[...])[0].astype(BF16)
    t_unit = unit(text_ref[...])[0].astype(BF16)
    t_all[pl.ds(t_base(0, 0, 0), SUB), :] = t_unit[:SUB]
    t_all[pl.ds(t_base(0, 0, 1), SUB), :] = t_unit[SUB:]
    labels[pl.ds(OWN * 8, 8), :] = jnp.broadcast_to(label_ref[...], (8, NR))

    row = lax.broadcasted_iota(jnp.int32, ids.shape, 0)
    k, core, which, j, r = row >> 9, (row >> 8) & 1, (row >> 7) & 1, (row >> 5) & 3, row & 31

    def shift_of(slot):
        return jnp.where(slot == 1, 3, jnp.where(slot == 2, 1, jnp.where(slot == 3, 2, 0)))

    dk, dj = shift_of(k), shift_of(j)
    row_y = (y + jnp.where(which == 0, dk, dj)) & 3
    row_x = (x + jnp.where(which == 0, dj, dk)) & 3
    row_c = c ^ core
    ids[...] = zh * 4096 + row_y * 1024 + row_x * 256 + zl * 128 + row_c * 64 + which * 32 + r

    pl.semaphore_wait(barrier, 7)

    start(("l", L1), ("l", R1), ("t1", 0, 1), ("t1", 0, 2), ("t1", 1, 1), ("t1", 1, 2))
    start(("s", L1, 0), ("s", R1, 1), ("s", L1, 1), ("s", R1, 0))
    for w in (0, 1):
        start(("t2", w, 1, 0), ("t2", w, 2, 0))
    t_back[...] = jnp.zeros_like(t_back)
    s_back[...] = jnp.zeros_like(s_back)
    for w in (0, 1):
        wait(("t1", w, 1))
        start(("t1", w, 3, 0), ("t2", w, 1, 1), ("t2", w, 2, 1))
        wait(("t1", w, 2))
        start(("t1", w, 3, 1), ("t2", w, 1, 2), ("t2", w, 2, 2))
    wait(("l", L1), ("l", R1))
    start(("l", L2), ("l", R2))
    wait(("s", L1, 0), ("s", R1, 1))
    start(("s", L2, 0), ("s", R2, 1))
    for w in (0, 1):
        wait(("t1", w, 3, 0), ("t1", w, 3, 1))
        start(("t2", w, 1, 3), ("t2", w, 2, 3), ("ts", w, 0))
    wait(("s", L1, 1), ("s", R1, 0))
    start(("s", L2, 1), ("s", R2, 0))
    for w in (0, 1):
        wait(("t2", w, 1, 0), ("t2", w, 1, 1))
        start(("t2", w, 3, 0))
        wait(("t2", w, 2, 2), ("t2", w, 2, 3))
        start(("t2", w, 3, 1))
    wait(("ts", 0, 0), ("ts", 1, 0))

    def before_1():
        for w in (0, 1):
            wait(("t2", w, 1, 2), ("t2", w, 1, 3))
            start(("ts", w, 1))
            wait(("t2", w, 2, 0), ("t2", w, 2, 1))
            start(("ts", w, 2))
        wait(("l", L2), ("l", R2))
        start(("l", L3), ("l", R3))
        wait(("s", L2, 0), ("s", R2, 1))
        start(("s", L3, 0), ("s", R3, 1))
        wait(("ts", 0, 1), ("ts", 1, 1))

    def before_2():
        wait(("ts", 0, 2), ("ts", 1, 2))
        for w in (0, 1):
            wait(("t2", w, 3, 0), ("t2", w, 3, 1))
            start(("ts", w, 3))

    def before_3():
        wait(("ts", 0, 3), ("ts", 1, 3))
        wait(("s", L2, 1), ("s", R2, 0))
        start(("s", L3, 1), ("s", R3, 0))

    def before_5():
        wait(("l", L3), ("l", R3))
        start(("l", D4))
        wait(("s", L3, 0), ("s", R3, 1))
        start(("s", D4, 0), ("s", D4, 1))

    def before_8():
        wait(("s", L3, 1), ("s", R3, 0))

    def before_12():
        wait(("s", D4, 0), ("s", D4, 1), ("l", D4))

    before = {1: before_1, 2: before_2, 3: before_3, 5: before_5, 8: before_8, 12: before_12}
    last_order = (3, 1, 2, 0)

    sharp = sharp_ref[0]
    shift = shift_ref[0]

    def one_chunk(i, carry):
        for when, act in before.items():
            pl.when(i == when)(act)
        u = i // 4
        n = i % 4
        k = jnp.where(u == 3, jnp.where(n == 0, 3, jnp.where(n == 3, 0, n)), n)
        first = pl.multiple_of(u * 256, 256)
        speech = s_all[pl.ds(first, 256), :]
        lab_pair = labels[pl.ds(pl.multiple_of(u * 16, 16), 16), :]
        part = jnp.zeros((256, E), F32)
        for half in range(2):
            rows = pl.ds(pl.multiple_of(k * CHUNK + half * 256, 256), 256)
            text = t_all[rows, :]
            logits = lax.dot_general(text, speech, (((1,), (1,)), ((), ())), preferred_element_type=F32)
            logits = sharp * logits + shift
            number = ids[rows, :]
            match = jnp.concatenate([number == lab_pair[0:1, :], number == lab_pair[8:9, :]], axis=1)
            coef = sharp * (1.0 / (1.0 + jnp.exp(-logits)) - match.astype(F32))
            coef = coef.astype(BF16)
            t_back[rows, :] += jnp.dot(coef, speech, preferred_element_type=F32)
            part += lax.dot_general(coef, text, (((0,), (0,)), ((), ())), preferred_element_type=F32)
        s_back[pl.ds(first, 256), :] += part
        for m, which_k in enumerate(last_order):
            pl.when(i == 12 + m)(functools.partial(start, ("sr", which_k)))
        return carry

    lax.fori_loop(0, 16, one_chunk, 0)

    def add(ref, other):
        ref[...] += other[...]

    start(("zr", 1, 0, 0), ("zr", -1, 0, 1), ("zr", 1, 1, 1), ("zr", -1, 1, 0))

    def merge_sibling(k):
        wait(("sr", k))
        add(t_back.at[pl.ds(t_base(k, 0, 0), 2 * SLAB)], sib_back.at[pl.ds(k * 2 * SLAB, 2 * SLAB)])

    merge_sibling(3)
    for w in (0, 1):
        start(("r2", w, 1, 0, 0), ("r2", w, -1, 0, 1))
    merge_sibling(2)
    for w in (0, 1):
        start(("r2", w, 1, 1, 1))
    merge_sibling(1)
    for w in (0, 1):
        start(("r2", w, -1, 1, 0))

    def z_step(order, half):
        for buf, chain, step in (
            (z_from_left, (D4, R3, R2, R1, OWN), 1), (z_from_right, (D4, L3, L2, L1, OWN), -1)
        ):
            h = half if step == 1 else 1 - half
            wait(("zr", step, order, h))
            add(sb(chain[order + 1], h), landing(buf, order, h))
            if order < 3:
                start(("zr", step, order + 1, h))

    for w in (0, 1):
        slab_at = lambda buf, order, half: buf.at[pl.ds(w * 256 + order * 128 + half * 64, 64)]
        wait(("r2", w, 1, 0, 0))
        add(tb(2, w, 0, 64), slab_at(slab_low, 0, 0))
        start(("r2", w, 1, 1, 0))
        wait(("r2", w, -1, 0, 1))
        add(tb(1, w, 64, 64), slab_at(slab_high, 0, 1))
        start(("r2", w, -1, 1, 1))
    merge_sibling(0)
    z_step(0, 0)
    z_step(1, 1)
    for w in (0, 1):
        slab_at = lambda buf, order, half: buf.at[pl.ds(w * 256 + order * 128 + half * 64, 64)]
        for half in (1, 0):
            wait(("r2", w, 1, 1, half), ("r2", w, -1, 1, half))
            ref = tb(0, w, half * 64, 64)
            ref[...] += slab_at(slab_low, 1, half)[...] + slab_at(slab_high, 1, half)[...]
        start(("r1", w, 1, 0, 0), ("r1", w, -1, 0, 1), ("r1", w, 1, 1, 1), ("r1", w, -1, 1, 0))
    z_step(1, 0)
    for w in (0, 1):
        sub_at = lambda buf, order, half: buf.at[pl.ds(w * 64 + order * 32 + half * 16, 16)]
        wait(("r1", w, 1, 0, 0))
        add(tb(0, w, 2 * SUB, 16), sub_at(sub_low, 0, 0))
        start(("r1", w, 1, 1, 0))
        wait(("r1", w, -1, 0, 1))
        add(tb(0, w, SUB + 16, 16), sub_at(sub_high, 0, 1))
        start(("r1", w, -1, 1, 1))
    z_step(2, 1)
    z_step(2, 0)
    for w in (0, 1):
        rows = pl.ds(w * SUB, SUB)
        for half in (0, 1):
            wait(("r1", w, 1, 1, half), ("r1", w, -1, 1, half))
        landed = pl.ds(w * 64 + 32, 32)
        back = tb(0, w, 0, SUB)[...] + sub_low[landed, :] + sub_high[landed, :]
        text_out[rows, :] = project(back, text_ref[rows, :])
    z_step(3, 1)
    z_step(3, 0)
    speech_out[...] = project(s_back[pl.ds(OWN * NR, NR), :], audio_ref[...])

    for done in copies.values():
        done.wait_send()
    assert len(copies) == COPIES


COPIES = 14 + 7 + 2 * (4 + 8 + 2 + 4) + 14 + 4 + 2 * 12


def shards(audio, sentence, matching, sharpness, offset):
    vmem = pl.BlockSpec(memory_space=pltpu.VMEM)
    smem = pl.BlockSpec(memory_space=pltpu.SMEM)
    return pl.pallas_call(
        kernel,
        out_shape=(jax.ShapeDtypeStruct((NR, E), F32), jax.ShapeDtypeStruct((NT, E), F32)),
        in_specs=[smem, smem, vmem, vmem, vmem],
        out_specs=(vmem, vmem),
        scratch_shapes=[
            pltpu.VMEM((8 * NR, E), BF16),
            pltpu.VMEM((4 * CHUNK, E), BF16),
            pltpu.VMEM((64, NR), jnp.int32),
            pltpu.VMEM((4 * CHUNK, 128), jnp.int32),
            pltpu.VMEM((4 * CHUNK, E), F32),
            pltpu.VMEM((8 * NR, E), F32),
            pltpu.VMEM((4 * NR, E), F32),
            pltpu.VMEM((4 * NR, E), F32),
            pltpu.VMEM((2 * CHUNK, E), F32),
            pltpu.VMEM((512, E), F32),
            pltpu.VMEM((512, E), F32),
            pltpu.VMEM((128, E), F32),
            pltpu.VMEM((128, E), F32),
            pltpu.SemaphoreType.DMA((COPIES,)),
            pltpu.SemaphoreType.DMA((COPIES,)),
        ],
        compiler_params=pltpu.CompilerParams(
            collective_id=0, has_side_effects=True, vmem_limit_bytes=60 * 1024 * 1024
        ),
    )(sharpness, offset, audio, sentence, matching.reshape(1, NR))


def solution(mesh):
    split = Mesh(mesh.devices.reshape(4, 4, 4, 2, 2), AXES)
    rows = P(AXES)
    return jax.shard_map(
        shards,
        mesh=split,
        in_specs=(rows, rows, rows, P(), P()),
        out_specs=(rows, rows),
        check_vma=False,
    )
```

time: 415 us -> 87.8 us (0.21)
  the two profiles are of different devices: /device:TPU:64 before, /device:TPU:1 now
where the time goes in v1:
time: 87.8 us; the launch traced here: 87.5 us
  Pallas kernels  83 us (95%)
  local copies, waits for them, and re-layouts  2.49 us (3%)
  between operations  1.94 us (2%)
    pallas_call x1, Pallas kernels, shards(): pl.pallas_call(kernel, out_shape=(jax.ShapeDtypeStruct((NR, E), F32), jax...  83 us
    unnamed x4, local copies, waits for them, and re-layouts  2.49 us

profile of v1, /device:TPU:1, one launch (start us, length us, event | category | flops | bytes accessed | tf_op | source)
XLA Modules:
  0.0 87.5 jit_solution(8378846001464598100)
XLA Ops:
  1.9 83.0 %shard_map.68 = (f32[128,768]{1,0:T(8,128)}, f32[64,768]{1,0:T(8,128)}) custom-call(f32[1]{0:T(128)S(6)} %copy.9.sharp_ref, f32[1]{0:T(128)S(6)} %copy.10.shift_ref, bf16[128,768]{1,0:T(8,128)(2,1)} %audio_ref.1, bf16[64,768]{1,0:T(8,128)(2,1)} %text_ref.1, s32[1,128]{1,0:T(1,128)} %bitcast.1), custom_call_target="tpu_custom_call" | custom-call | tf_op jit(solution)/shard_map/pallas_call | solution.py:354
  85.0 0.0 copy-start
  85.0 1.8 %copy.11 = f32[128,768]{1,0:T(8,128)} copy(f32[128,768]{1,0:T(8,128)} %get-tuple-element.4) | data formatting | bytes 786432
  86.8 0.0 copy-done
  86.8 0.7 copy.12
Async XLA Ops:
  85.0 1.8 %copy-start = (f32[64,768]{1,0:T(8,128)S(1)}, f32[64,768]{1,0:T(8,128)}, u32[]{:S(2)}) copy-start(f32[64,768]{1,0:T(8,128)} %get-tuple-element.5) | copy-start | bytes 589828

commit v2 on v1

--- a/solution.py
+++ b/solution.py
@@ -38,7 +38,7 @@
     speech_out, text_out,
     s_all, t_all, labels, ids, t_back, s_back,
     z_from_left, z_from_right, sib_back, slab_low, slab_high, sub_low, sub_high,
-    send_sems, recv_sems,
+    coef_even, coef_odd, send_sems, recv_sems,
 ):
     zh, y, x, zl, c = (lax.axis_index(a) for a in AXES)
     z = zh * 2 + zl
@@ -202,26 +202,28 @@
         start(("t2", w, 3, 1))
     wait(("ts", 0, 0), ("ts", 1, 0))
 
-    def before_1():
+    def before_0():
         for w in (0, 1):
             wait(("t2", w, 1, 2), ("t2", w, 1, 3))
             start(("ts", w, 1))
             wait(("t2", w, 2, 0), ("t2", w, 2, 1))
             start(("ts", w, 2))
+        wait(("ts", 0, 1), ("ts", 1, 1))
+
+    def before_1():
+        wait(("ts", 0, 2), ("ts", 1, 2))
         wait(("l", L2), ("l", R2))
         start(("l", L3), ("l", R3))
         wait(("s", L2, 0), ("s", R2, 1))
         start(("s", L3, 0), ("s", R3, 1))
-        wait(("ts", 0, 1), ("ts", 1, 1))
-
-    def before_2():
-        wait(("ts", 0, 2), ("ts", 1, 2))
         for w in (0, 1):
             wait(("t2", w, 3, 0), ("t2", w, 3, 1))
             start(("ts", w, 3))
 
+    def before_2():
+        wait(("ts", 0, 3), ("ts", 1, 3))
+
     def before_3():
-        wait(("ts", 0, 3), ("ts", 1, 3))
         wait(("s", L2, 1), ("s", R2, 0))
         start(("s", L3, 1), ("s", R3, 0))
 
@@ -231,64 +233,94 @@
         wait(("s", L3, 0), ("s", R3, 1))
         start(("s", D4, 0), ("s", D4, 1))
 
-    def before_8():
+    def before_7():
         wait(("s", L3, 1), ("s", R3, 0))
 
+    def before_11():
+        wait(("s", D4, 0), ("s", D4, 1), ("l", D4))
+
     def before_12():
-        wait(("s", D4, 0), ("s", D4, 1), ("l", D4))
-
-    before = {1: before_1, 2: before_2, 3: before_3, 5: before_5, 8: before_8, 12: before_12}
-    last_order = (3, 1, 2, 0)
+        start(("zr", 1, 1, 1), ("zr", -1, 1, 0))
+
+    def before_13():
+        start(("sr", 3))
+
+    before = {
+        0: before_0, 1: before_1, 2: before_2, 3: before_3, 5: before_5, 7: before_7, 11: before_11,
+        12: before_12, 13: before_13,
+    }
 
     sharp = sharp_ref[0]
     shift = shift_ref[0]
 
-    def one_chunk(i, carry):
-        for when, act in before.items():
-            pl.when(i == when)(act)
+    def place(i):
         u = i // 4
         n = i % 4
         k = jnp.where(u == 3, jnp.where(n == 0, 3, jnp.where(n == 3, 0, n)), n)
-        first = pl.multiple_of(u * 256, 256)
-        speech = s_all[pl.ds(first, 256), :]
-        lab_pair = labels[pl.ds(pl.multiple_of(u * 16, 16), 16), :]
-        part = jnp.zeros((256, E), F32)
+        return pl.multiple_of(u * 256, 256), pl.multiple_of(k * CHUNK, CHUNK), pl.multiple_of(u * 16, 16)
+
+    def forward(i, coefs):
+        s0, t0, l0 = place(i)
+        speech = s_all[pl.ds(s0, 256), :]
+        lab_pair = labels[pl.ds(l0, 16), :]
         for half in range(2):
-            rows = pl.ds(pl.multiple_of(k * CHUNK + half * 256, 256), 256)
-            text = t_all[rows, :]
-            logits = lax.dot_general(text, speech, (((1,), (1,)), ((), ())), preferred_element_type=F32)
+            rows = pl.ds(pl.multiple_of(t0 + half * 256, 256), 256)
+            logits = lax.dot_general(
+                t_all[rows, :], speech, (((1,), (1,)), ((), ())), preferred_element_type=F32
+            )
             logits = sharp * logits + shift
             number = ids[rows, :]
             match = jnp.concatenate([number == lab_pair[0:1, :], number == lab_pair[8:9, :]], axis=1)
             coef = sharp * (1.0 / (1.0 + jnp.exp(-logits)) - match.astype(F32))
-            coef = coef.astype(BF16)
-            t_back[rows, :] += jnp.dot(coef, speech, preferred_element_type=F32)
-            part += lax.dot_general(coef, text, (((0,), (0,)), ((), ())), preferred_element_type=F32)
-        s_back[pl.ds(first, 256), :] += part
-        for m, which_k in enumerate(last_order):
-            pl.when(i == 12 + m)(functools.partial(start, ("sr", which_k)))
+            coefs[pl.ds(half * 256, 256), :] = coef.astype(BF16)
+
+    def backward(i, coefs):
+        s0, t0, _ = place(i)
+        coef = coefs[...]
+        rows = pl.ds(t0, CHUNK)
+        s_back[pl.ds(s0, 256), :] += lax.dot_general(
+            coef, t_all[rows, :], (((0,), (0,)), ((), ())), preferred_element_type=F32
+        )
+        t_back[rows, :] += jnp.dot(coef, s_all[pl.ds(s0, 256), :], preferred_element_type=F32)
+
+    forward(0, coef_even)
+
+    def two_chunks(h, carry):
+        for parity, ready, filled in ((0, coef_even, coef_odd), (1, coef_odd, coef_even)):
+            for when, act in before.items():
+                if when % 2 == parity:
+                    pl.when(h == when // 2)(act)
+            i = h * 2 + parity
+            forward(i + 1, filled)
+            backward(i, ready)
         return carry
 
-    lax.fori_loop(0, 16, one_chunk, 0)
+    lax.fori_loop(0, 7, two_chunks, 0)
 
     def add(ref, other):
         ref[...] += other[...]
-
-    start(("zr", 1, 0, 0), ("zr", -1, 0, 1), ("zr", 1, 1, 1), ("zr", -1, 1, 0))
 
     def merge_sibling(k):
         wait(("sr", k))
         add(t_back.at[pl.ds(t_base(k, 0, 0), 2 * SLAB)], sib_back.at[pl.ds(k * 2 * SLAB, 2 * SLAB)])
 
+    start(("sr", 1))
+    forward(15, coef_odd)
+    backward(14, coef_even)
+    start(("sr", 2))
     merge_sibling(3)
     for w in (0, 1):
         start(("r2", w, 1, 0, 0), ("r2", w, -1, 0, 1))
+    merge_sibling(1)
+    for w in (0, 1):
+        start(("r2", w, -1, 1, 0))
+    backward(15, coef_odd)
+    start(("sr", 0))
+
+    start(("zr", 1, 0, 0), ("zr", -1, 0, 1))
     merge_sibling(2)
     for w in (0, 1):
         start(("r2", w, 1, 1, 1))
-    merge_sibling(1)
-    for w in (0, 1):
-        start(("r2", w, -1, 1, 0))
 
     def z_step(order, half):
         for buf, chain, step in (
@@ -370,6 +402,8 @@
             pltpu.VMEM((512, E), F32),
             pltpu.VMEM((128, E), F32),
             pltpu.VMEM((128, E), F32),
+            pltpu.VMEM((CHUNK, 256), BF16),
+            pltpu.VMEM((CHUNK, 256), BF16),
             pltpu.SemaphoreType.DMA((COPIES,)),
             pltpu.SemaphoreType.DMA((COPIES,)),
         ],

time: 87.8 us -> 79.9 us (0.910)
  Pallas kernels: 83 us -> 75.1 us
    pallas_call x1, Pallas kernels: 83 us -> 75.1 us  [shards(): pl.pallas_call(kernel, out_shape=(jax.ShapeDtypeStruct((NR, E), F32), jax...]
where the time goes in v2:
time: 79.9 us; the launch traced here: 79.5 us
  Pallas kernels  75.1 us (94%)
  local copies, waits for them, and re-layouts  2.49 us (3%)
  between operations  1.94 us (2%)
    pallas_call x1, Pallas kernels, shards(): pl.pallas_call(kernel, out_shape=(jax.ShapeDtypeStruct((NR, E), F32), jax...  75.1 us
    unnamed x4, local copies, waits for them, and re-layouts  2.49 us

profile of v2, /device:TPU:1, one launch (start us, length us, event | category | flops | bytes accessed | tf_op | source)
XLA Modules:
  0.0 79.5 jit_solution(51657510039626744)
XLA Ops:
  1.9 75.1 %shard_map.68 = (f32[128,768]{1,0:T(8,128)}, f32[64,768]{1,0:T(8,128)}) custom-call(f32[1]{0:T(128)S(6)} %copy.9.sharp_ref, f32[1]{0:T(128)S(6)} %copy.10.shift_ref, bf16[128,768]{1,0:T(8,128)(2,1)} %audio_ref.1, bf16[64,768]{1,0:T(8,128)(2,1)} %text_ref.1, s32[1,128]{1,0:T(1,128)} %bitcast.1), custom_call_target="tpu_custom_call" | custom-call | tf_op jit(solution)/shard_map/pallas_call | solution.py:386
  77.0 0.0 copy-start
  77.0 1.8 %copy.11 = f32[128,768]{1,0:T(8,128)} copy(f32[128,768]{1,0:T(8,128)} %get-tuple-element.4) | data formatting | bytes 786432
  78.8 0.0 copy-done
  78.8 0.7 copy.12
Async XLA Ops:
  77.0 1.8 %copy-start = (f32[64,768]{1,0:T(8,128)S(1)}, f32[64,768]{1,0:T(8,128)}, u32[]{:S(2)}) copy-start(f32[64,768]{1,0:T(8,128)} %get-tuple-element.5) | copy-start | bytes 589828

commit v3 on v2

--- a/solution.py
+++ b/solution.py
@@ -16,6 +16,7 @@
 L1, R1, L2, R2, L3, R3, OWN, D4 = range(8)
 NR, NT, E = 128, 64, 768
 HALF = NR // 2
+PIECE = NR // 4
 SLAB = 128
 SUB = 32
 CHUNK = 512
@@ -37,7 +38,7 @@
     sharp_ref, shift_ref, audio_ref, text_ref, label_ref,
     speech_out, text_out,
     s_all, t_all, labels, ids, t_back, s_back,
-    z_from_left, z_from_right, sib_back, slab_low, slab_high, sub_low, sub_high,
+    sib_back, q_out, q_in, scale_out, scale_in,
     coef_even, coef_odd, send_sems, recv_sems,
 ):
     zh, y, x, zl, c = (lax.axis_index(a) for a in AXES)
@@ -110,20 +111,49 @@
         for k in range(4):
             copy(("ts", w, k), t_rows(k, 0, w, 0, SLAB), t_rows(k, 1, w, 0, SLAB), sibling)
 
-    def sb(slot, half):
-        return s_back.at[pl.ds(slot * NR + half * HALF, HALF)]
-
-    def landing(buf, order, half):
-        return buf.at[pl.ds((order * 2 + half) * HALF, HALF)]
-
-    for buf, chain, step, d4half in (
-        (z_from_left, (D4, R3, R2, R1, OWN), 1, 0), (z_from_right, (D4, L3, L2, L1, OWN), -1, 1)
-    ):
+    routes = {}
+    used = [0]
+
+    def route(name, ref, rows, device):
+        first, n = used[0], len(routes)
+        used[0] += rows
+        into = (q_in.at[pl.ds(first, rows)], scale_in.at[pl.ds(n * 8, 8)])
+        out = (q_out.at[pl.ds(first, rows)], scale_out.at[pl.ds(n * 8, 8)])
+        routes[name] = (ref, rows, out, into)
+        for what, src, dst in zip("sq", reversed(out), reversed(into)):
+            copy((*name, what), src, dst, device)
+
+    def ship(*names):
+        for name in names:
+            ref, rows, (numbers, scales), _ = routes[name]
+            value = ref[...]
+            top = jnp.maximum(jnp.max(jnp.abs(value), axis=1, keepdims=True), 1e-30)
+            numbers[...] = jnp.round(value * (32767.0 / top)).astype(jnp.int16)
+            scale = top * (1.0 / 32767.0)
+            lane = lax.broadcasted_iota(jnp.int32, (8, 128), 1)
+            tile = jnp.zeros((8, 128), F32)
+            for v in range(rows // 8):
+                tile = jnp.where(lane == v, scale[v * 8 : v * 8 + 8], tile)
+            scales[...] = tile
+            start((*name, "s"), (*name, "q"))
+
+    def landed(name):
+        _, rows, _, (numbers, scales) = routes[name]
+        wait((*name, "s"), (*name, "q"))
+        tile = scales[...]
+        scale = jnp.concatenate([tile[:, v : v + 1] for v in range(rows // 8)], axis=0)
+        return numbers[...].astype(F32) * scale
+
+    def sb(slot, piece):
+        return s_back.at[pl.ds(slot * NR + piece * PIECE, PIECE)]
+
+    chains = {1: (D4, R3, R2, R1, OWN), -1: (D4, L3, L2, L1, OWN)}
+    far_pieces = {1: (0, 1), -1: (2, 3)}
+    for step, chain in chains.items():
         for order, src in enumerate(chain[:-1]):
-            for half in (0, 1):
-                if src == D4 and half != d4half:
-                    continue
-                copy(("zr", step, order, half), sb(src, half), landing(buf, order, half), at_z(step))
+            for piece in range(4):
+                if src != D4 or piece in far_pieces[step]:
+                    route(("zr", step, order, piece), sb(src, piece), PIECE, at_z(step))
 
     def tb(k, which, first, count):
         return t_back.at[pl.ds(t_base(k, 0, which) + first, count)]
@@ -134,22 +164,14 @@
             sib_back.at[pl.ds(k * 2 * SLAB, 2 * SLAB)], sibling,
         )
     for w, (first, second) in enumerate(((at_x, at_y), (at_y, at_x))):
-        slab_at = lambda buf, order, half: buf.at[pl.ds(w * 256 + order * 128 + half * 64, 64)]
-        sub_at = lambda buf, order, half: buf.at[pl.ds(w * 64 + order * 32 + half * 16, 16)]
-        for buf, k, step, d2half in ((slab_low, 2, 1, 0), (slab_high, 1, -1, 1)):
-            copy(("r2", w, step, 0, d2half), tb(3, w, d2half * 64, 64), slab_at(buf, 0, d2half), second(step))
+        for k, step, far in ((2, 1, 0), (1, -1, 1)):
+            route(("r2", w, step, 0, far), tb(3, w, far * 64, 64), 64, second(step))
             for half in (0, 1):
-                copy(("r2", w, step, 1, half), tb(k, w, half * 64, 64), slab_at(buf, 1, half), second(step))
-        for buf, j, step, d2half in ((sub_low, 2, 1, 0), (sub_high, 1, -1, 1)):
-            copy(
-                ("r1", w, step, 0, d2half), tb(0, w, 3 * SUB + d2half * 16, 16),
-                sub_at(buf, 0, d2half), first(step),
-            )
+                route(("r2", w, step, 1, half), tb(k, w, half * 64, 64), 64, second(step))
+        for j, step, far in ((2, 1, 0), (1, -1, 1)):
+            route(("r1", w, step, 0, far), tb(0, w, 3 * SUB + far * 16, 16), 16, first(step))
             for half in (0, 1):
-                copy(
-                    ("r1", w, step, 1, half), tb(0, w, j * SUB + half * 16, 16),
-                    sub_at(buf, 1, half), first(step),
-                )
+                route(("r1", w, step, 1, half), tb(0, w, j * SUB + half * 16, 16), 16, first(step))
 
     barrier = pltpu.get_barrier_semaphore()
     for device in (at_z(1), at_z(-1), at_y(1), at_y(-1), at_x(1), at_x(-1), sibling):
@@ -175,8 +197,8 @@
 
     pl.semaphore_wait(barrier, 7)
 
-    start(("l", L1), ("l", R1), ("t1", 0, 1), ("t1", 0, 2), ("t1", 1, 1), ("t1", 1, 2))
-    start(("s", L1, 0), ("s", R1, 1), ("s", L1, 1), ("s", R1, 0))
+    start(("s", L1, 0), ("s", R1, 1), ("t1", 0, 1), ("t1", 0, 2), ("t1", 1, 1), ("t1", 1, 2))
+    start(("l", L1), ("l", R1), ("s", L1, 1), ("s", R1, 0))
     for w in (0, 1):
         start(("t2", w, 1, 0), ("t2", w, 2, 0))
     t_back[...] = jnp.zeros_like(t_back)
@@ -186,52 +208,47 @@
         start(("t1", w, 3, 0), ("t2", w, 1, 1), ("t2", w, 2, 1))
         wait(("t1", w, 2))
         start(("t1", w, 3, 1), ("t2", w, 1, 2), ("t2", w, 2, 2))
+    wait(("s", L1, 0), ("s", R1, 1))
+    start(("s", L2, 0), ("s", R2, 1))
     wait(("l", L1), ("l", R1))
     start(("l", L2), ("l", R2))
-    wait(("s", L1, 0), ("s", R1, 1))
-    start(("s", L2, 0), ("s", R2, 1))
     for w in (0, 1):
         wait(("t1", w, 3, 0), ("t1", w, 3, 1))
         start(("t2", w, 1, 3), ("t2", w, 2, 3), ("ts", w, 0))
+    for w in (0, 1):
+        wait(("t2", w, 1, 0), ("t2", w, 1, 1))
+        start(("t2", w, 3, 0))
     wait(("s", L1, 1), ("s", R1, 0))
     start(("s", L2, 1), ("s", R2, 0))
-    for w in (0, 1):
-        wait(("t2", w, 1, 0), ("t2", w, 1, 1))
-        start(("t2", w, 3, 0))
-        wait(("t2", w, 2, 2), ("t2", w, 2, 3))
-        start(("t2", w, 3, 1))
     wait(("ts", 0, 0), ("ts", 1, 0))
 
     def before_0():
+        for w in (0, 1):
+            wait(("t2", w, 2, 2), ("t2", w, 2, 3))
+            start(("t2", w, 3, 1))
         for w in (0, 1):
             wait(("t2", w, 1, 2), ("t2", w, 1, 3))
             start(("ts", w, 1))
             wait(("t2", w, 2, 0), ("t2", w, 2, 1))
             start(("ts", w, 2))
+        wait(("s", L2, 0), ("s", R2, 1), ("l", L2), ("l", R2))
+        start(("s", L3, 0), ("s", R3, 1), ("l", L3), ("l", R3))
         wait(("ts", 0, 1), ("ts", 1, 1))
 
     def before_1():
         wait(("ts", 0, 2), ("ts", 1, 2))
-        wait(("l", L2), ("l", R2))
-        start(("l", L3), ("l", R3))
-        wait(("s", L2, 0), ("s", R2, 1))
-        start(("s", L3, 0), ("s", R3, 1))
         for w in (0, 1):
             wait(("t2", w, 3, 0), ("t2", w, 3, 1))
             start(("ts", w, 3))
 
     def before_2():
-        wait(("ts", 0, 3), ("ts", 1, 3))
-
-    def before_3():
         wait(("s", L2, 1), ("s", R2, 0))
         start(("s", L3, 1), ("s", R3, 0))
-
-    def before_5():
-        wait(("l", L3), ("l", R3))
-        start(("l", D4))
-        wait(("s", L3, 0), ("s", R3, 1))
-        start(("s", D4, 0), ("s", D4, 1))
+        wait(("ts", 0, 3), ("ts", 1, 3))
+
+    def before_4():
+        wait(("s", L3, 0), ("s", R3, 1), ("l", L3), ("l", R3))
+        start(("s", D4, 0), ("s", D4, 1), ("l", D4))
 
     def before_7():
         wait(("s", L3, 1), ("s", R3, 0))
@@ -240,13 +257,14 @@
         wait(("s", D4, 0), ("s", D4, 1), ("l", D4))
 
     def before_12():
-        start(("zr", 1, 1, 1), ("zr", -1, 1, 0))
+        for step, pieces in ((1, (2, 3)), (-1, (0, 1))):
+            ship(*(("zr", step, 1, piece) for piece in pieces))
 
     def before_13():
         start(("sr", 3))
 
     before = {
-        0: before_0, 1: before_1, 2: before_2, 3: before_3, 5: before_5, 7: before_7, 11: before_11,
+        0: before_0, 1: before_1, 2: before_2, 4: before_4, 7: before_7, 11: before_11,
         12: before_12, 13: before_13,
     }
 
@@ -304,80 +322,74 @@
         wait(("sr", k))
         add(t_back.at[pl.ds(t_base(k, 0, 0), 2 * SLAB)], sib_back.at[pl.ds(k * 2 * SLAB, 2 * SLAB)])
 
+    def z_step(order, pieces):
+        for p in pieces:
+            for step, chain in chains.items():
+                piece = p if step == 1 else (p + 2) % 4
+                ref = sb(chain[order + 1], piece)
+                ref[...] += landed(("zr", step, order, piece))
+                if order < 3:
+                    ship(("zr", step, order + 1, piece))
+
     start(("sr", 1))
     forward(15, coef_odd)
     backward(14, coef_even)
     start(("sr", 2))
     merge_sibling(3)
     for w in (0, 1):
-        start(("r2", w, 1, 0, 0), ("r2", w, -1, 0, 1))
-    merge_sibling(1)
-    for w in (0, 1):
-        start(("r2", w, -1, 1, 0))
+        ship(("r2", w, 1, 0, 0), ("r2", w, -1, 0, 1))
     backward(15, coef_odd)
     start(("sr", 0))
-
-    start(("zr", 1, 0, 0), ("zr", -1, 0, 1))
+    ship(("zr", 1, 0, 0), ("zr", -1, 0, 2), ("zr", 1, 0, 1), ("zr", -1, 0, 3))
+    merge_sibling(1)
+    for w in (0, 1):
+        ship(("r2", w, -1, 1, 0))
     merge_sibling(2)
     for w in (0, 1):
-        start(("r2", w, 1, 1, 1))
-
-    def z_step(order, half):
-        for buf, chain, step in (
-            (z_from_left, (D4, R3, R2, R1, OWN), 1), (z_from_right, (D4, L3, L2, L1, OWN), -1)
-        ):
-            h = half if step == 1 else 1 - half
-            wait(("zr", step, order, h))
-            add(sb(chain[order + 1], h), landing(buf, order, h))
-            if order < 3:
-                start(("zr", step, order + 1, h))
-
-    for w in (0, 1):
-        slab_at = lambda buf, order, half: buf.at[pl.ds(w * 256 + order * 128 + half * 64, 64)]
-        wait(("r2", w, 1, 0, 0))
-        add(tb(2, w, 0, 64), slab_at(slab_low, 0, 0))
-        start(("r2", w, 1, 1, 0))
-        wait(("r2", w, -1, 0, 1))
-        add(tb(1, w, 64, 64), slab_at(slab_high, 0, 1))
-        start(("r2", w, -1, 1, 1))
+        ship(("r2", w, 1, 1, 1))
+    z_step(1, (2, 3))
+    z_step(0, (0, 1))
+    for w in (0, 1):
+        ref = tb(2, w, 0, 64)
+        ref[...] += landed(("r2", w, 1, 0, 0))
+        ship(("r2", w, 1, 1, 0))
+        ref = tb(1, w, 64, 64)
+        ref[...] += landed(("r2", w, -1, 0, 1))
+        ship(("r2", w, -1, 1, 1))
     merge_sibling(0)
-    z_step(0, 0)
-    z_step(1, 1)
-    for w in (0, 1):
-        slab_at = lambda buf, order, half: buf.at[pl.ds(w * 256 + order * 128 + half * 64, 64)]
-        for half in (1, 0):
-            wait(("r2", w, 1, 1, half), ("r2", w, -1, 1, half))
+    z_step(2, (2, 3))
+    z_step(1, (0, 1))
+    for w in (0, 1):
+        for half, step in ((1, 1), (0, -1), (0, 1), (1, -1)):
             ref = tb(0, w, half * 64, 64)
-            ref[...] += slab_at(slab_low, 1, half)[...] + slab_at(slab_high, 1, half)[...]
-        start(("r1", w, 1, 0, 0), ("r1", w, -1, 0, 1), ("r1", w, 1, 1, 1), ("r1", w, -1, 1, 0))
-    z_step(1, 0)
-    for w in (0, 1):
-        sub_at = lambda buf, order, half: buf.at[pl.ds(w * 64 + order * 32 + half * 16, 16)]
-        wait(("r1", w, 1, 0, 0))
-        add(tb(0, w, 2 * SUB, 16), sub_at(sub_low, 0, 0))
-        start(("r1", w, 1, 1, 0))
-        wait(("r1", w, -1, 0, 1))
-        add(tb(0, w, SUB + 16, 16), sub_at(sub_high, 0, 1))
-        start(("r1", w, -1, 1, 1))
-    z_step(2, 1)
-    z_step(2, 0)
-    for w in (0, 1):
+            ref[...] += landed(("r2", w, step, 1, half))
+        ship(("r1", w, 1, 0, 0), ("r1", w, -1, 0, 1), ("r1", w, 1, 1, 1), ("r1", w, -1, 1, 0))
+    z_step(2, (0, 1))
+    for w in (0, 1):
+        ref = tb(0, w, 2 * SUB, 16)
+        ref[...] += landed(("r1", w, 1, 0, 0))
+        ship(("r1", w, 1, 1, 0))
+        ref = tb(0, w, SUB + 16, 16)
+        ref[...] += landed(("r1", w, -1, 0, 1))
+        ship(("r1", w, -1, 1, 1))
+    z_step(3, (2, 3))
+    for w in (0, 1):
+        for half in (0, 1):
+            ref = tb(0, w, half * 16, 16)
+            ref[...] += landed(("r1", w, 1, 1, half)) + landed(("r1", w, -1, 1, half))
         rows = pl.ds(w * SUB, SUB)
-        for half in (0, 1):
-            wait(("r1", w, 1, 1, half), ("r1", w, -1, 1, half))
-        landed = pl.ds(w * 64 + 32, 32)
-        back = tb(0, w, 0, SUB)[...] + sub_low[landed, :] + sub_high[landed, :]
-        text_out[rows, :] = project(back, text_ref[rows, :])
-    z_step(3, 1)
-    z_step(3, 0)
+        text_out[rows, :] = project(tb(0, w, 0, SUB)[...], text_ref[rows, :])
+    z_step(3, (0, 1))
     speech_out[...] = project(s_back[pl.ds(OWN * NR, NR), :], audio_ref[...])
 
     for done in copies.values():
         done.wait_send()
-    assert len(copies) == COPIES
-
-
-COPIES = 14 + 7 + 2 * (4 + 8 + 2 + 4) + 14 + 4 + 2 * 12
+    assert len(copies) == COPIES and len(routes) == ROUTES and used[0] == Q_ROWS
+
+
+ROUTES = 28 + 12 + 12
+Q_ROWS = 28 * PIECE + 12 * 64 + 12 * 16
+COPIES = 14 + 7 + 2 * (4 + 8 + 2 + 4) + 4 + 2 * ROUTES
 
 
 def shards(audio, sentence, matching, sharpness, offset):
@@ -395,13 +407,11 @@
             pltpu.VMEM((4 * CHUNK, 128), jnp.int32),
             pltpu.VMEM((4 * CHUNK, E), F32),
             pltpu.VMEM((8 * NR, E), F32),
-            pltpu.VMEM((4 * NR, E), F32),
-            pltpu.VMEM((4 * NR, E), F32),
             pltpu.VMEM((2 * CHUNK, E), F32),
-            pltpu.VMEM((512, E), F32),
-            pltpu.VMEM((512, E), F32),
-            pltpu.VMEM((128, E), F32),
-            pltpu.VMEM((128, E), F32),
+            pltpu.VMEM((Q_ROWS, E), jnp.int16),
+            pltpu.VMEM((Q_ROWS, E), jnp.int16),
+            pltpu.VMEM((8 * ROUTES, 128), F32),
+            pltpu.VMEM((8 * ROUTES, 128), F32),
             pltpu.VMEM((CHUNK, 256), BF16),
             pltpu.VMEM((CHUNK, 256), BF16),
             pltpu.SemaphoreType.DMA((COPIES,)),

time: 79.9 us -> 70.1 us (0.88)
  Pallas kernels: 75.1 us -> 65.5 us
    pallas_call x1, Pallas kernels: 75.1 us -> 65.5 us  [shards(): pl.pallas_call(kernel, out_shape=(jax.ShapeDtypeStruct((NR, E), F32), jax...]
where the time goes in v3:
time: 70.1 us; the launch traced here: 70 us
  Pallas kernels  65.5 us (93%)
  local copies, waits for them, and re-layouts  2.49 us (4%)
  between operations  1.94 us (3%)
    pallas_call x1, Pallas kernels, shards(): pl.pallas_call(kernel, out_shape=(jax.ShapeDtypeStruct((NR, E), F32), jax...  65.5 us
    unnamed x4, local copies, waits for them, and re-layouts  2.49 us

profile of v3, /device:TPU:1, one launch (start us, length us, event | category | flops | bytes accessed | tf_op | source)
XLA Modules:
  0.0 70.0 jit_solution(6384642832736036871)
XLA Ops:
  1.9 65.5 %shard_map.68 = (f32[128,768]{1,0:T(8,128)}, f32[64,768]{1,0:T(8,128)}) custom-call(f32[1]{0:T(128)S(6)} %copy.9.sharp_ref, f32[1]{0:T(128)S(6)} %copy.10.shift_ref, bf16[128,768]{1,0:T(8,128)(2,1)} %audio_ref.1, bf16[64,768]{1,0:T(8,128)(2,1)} %text_ref.1, s32[1,128]{1,0:T(1,128)} %bitcast.1), custom_call_target="tpu_custom_call" | custom-call | tf_op jit(solution)/shard_map/pallas_call | solution.py:398
  67.5 0.0 copy-start
  67.5 1.8 %copy.11 = f32[128,768]{1,0:T(8,128)} copy(f32[128,768]{1,0:T(8,128)} %get-tuple-element.4) | data formatting | bytes 786432
  69.3 0.0 copy-done
  69.3 0.7 copy.12
Async XLA Ops:
  67.5 1.8 %copy-start = (f32[64,768]{1,0:T(8,128)S(1)}, f32[64,768]{1,0:T(8,128)}, u32[]{:S(2)}) copy-start(f32[64,768]{1,0:T(8,128)} %get-tuple-element.5) | copy-start | bytes 589828

commit v4 on v3

--- a/solution.py
+++ b/solution.py
@@ -99,15 +99,10 @@
 
     for w, (first, second) in enumerate(((at_x, at_y), (at_y, at_x))):
         piece = lambda j, lo=0, n=SUB: t_rows(0, 0, w, j * SUB + lo, n)
-        copy(("t1", w, 1), piece(0), piece(1), first(1))
-        copy(("t1", w, 2), piece(0), piece(2), first(-1))
-        copy(("t1", w, 3, 0), piece(1, 0, 16), piece(3, 0, 16), first(1))
-        copy(("t1", w, 3, 1), piece(2, 16, 16), piece(3, 16, 16), first(-1))
-        for j in range(4):
-            copy(("t2", w, 1, j), piece(j), t_rows(1, 0, w, j * SUB, SUB), second(1))
-            copy(("t2", w, 2, j), piece(j), t_rows(2, 0, w, j * SUB, SUB), second(-1))
-        copy(("t2", w, 3, 0), t_rows(1, 0, w, 0, 64), t_rows(3, 0, w, 0, 64), second(1))
-        copy(("t2", w, 3, 1), t_rows(2, 0, w, 64, 64), t_rows(3, 0, w, 64, 64), second(-1))
+        for slot, step in ((1, 1), (2, -1), (3, 2)):
+            copy(("t1", w, slot), piece(0), piece(slot), first(step))
+            for j in range(4):
+                copy(("t2", w, slot, j), piece(j), t_rows(slot, 0, w, j * SUB, SUB), second(step))
         for k in range(4):
             copy(("ts", w, k), t_rows(k, 0, w, 0, SLAB), t_rows(k, 1, w, 0, SLAB), sibling)
 
@@ -123,23 +118,38 @@
         for what, src, dst in zip("sq", reversed(out), reversed(into)):
             copy((*name, what), src, dst, device)
 
+    def pack(name, value):
+        _, rows, (numbers, scales), _ = routes[name]
+        top = jnp.maximum(jnp.max(jnp.abs(value), axis=1, keepdims=True), 1e-30)
+        numbers[...] = jnp.round(value * (32767.0 / top)).astype(jnp.int16)
+        scale = top * (1.0 / 32767.0)
+        lane = lax.broadcasted_iota(jnp.int32, (8, 128), 1)
+        tile = jnp.zeros((8, 128), F32)
+        for v in range(rows // 8):
+            tile = jnp.where(lane == v, scale[v * 8 : v * 8 + 8], tile)
+        scales[...] = tile
+
+    def send(*names):
+        for name in names:
+            start((*name, "s"), (*name, "q"))
+
     def ship(*names):
         for name in names:
-            ref, rows, (numbers, scales), _ = routes[name]
-            value = ref[...]
-            top = jnp.maximum(jnp.max(jnp.abs(value), axis=1, keepdims=True), 1e-30)
-            numbers[...] = jnp.round(value * (32767.0 / top)).astype(jnp.int16)
-            scale = top * (1.0 / 32767.0)
-            lane = lax.broadcasted_iota(jnp.int32, (8, 128), 1)
-            tile = jnp.zeros((8, 128), F32)
-            for v in range(rows // 8):
-                tile = jnp.where(lane == v, scale[v * 8 : v * 8 + 8], tile)
-            scales[...] = tile
-            start((*name, "s"), (*name, "q"))
-
-    def landed(name):
+            pack(name, routes[name][0][...])
+        send(*names)
+
+    def arrived(*names):
+        for name in names:
+            wait((*name, "s"), (*name, "q"))
+
+    def forward_sum(*pairs):
+        arrived(*(come for come, _ in pairs))
+        for come, leave in pairs:
+            pack(leave, routes[leave][0][...] + unpacked(come))
+        send(*(leave for _, leave in pairs))
+
+    def unpacked(name):
         _, rows, _, (numbers, scales) = routes[name]
-        wait((*name, "s"), (*name, "q"))
         tile = scales[...]
         scale = jnp.concatenate([tile[:, v : v + 1] for v in range(rows // 8)], axis=0)
         return numbers[...].astype(F32) * scale
@@ -164,17 +174,13 @@
             sib_back.at[pl.ds(k * 2 * SLAB, 2 * SLAB)], sibling,
         )
     for w, (first, second) in enumerate(((at_x, at_y), (at_y, at_x))):
-        for k, step, far in ((2, 1, 0), (1, -1, 1)):
-            route(("r2", w, step, 0, far), tb(3, w, far * 64, 64), 64, second(step))
+        for slot, step in ((3, 2), (2, 1), (1, -1)):
             for half in (0, 1):
-                route(("r2", w, step, 1, half), tb(k, w, half * 64, 64), 64, second(step))
-        for j, step, far in ((2, 1, 0), (1, -1, 1)):
-            route(("r1", w, step, 0, far), tb(0, w, 3 * SUB + far * 16, 16), 16, first(step))
-            for half in (0, 1):
-                route(("r1", w, step, 1, half), tb(0, w, j * SUB + half * 16, 16), 16, first(step))
+                route(("r2", w, slot, half), tb(slot, w, half * 64, 64), 64, second(step))
+            route(("r1", w, slot), tb(0, w, slot * SUB, SUB), SUB, first(step))
 
     barrier = pltpu.get_barrier_semaphore()
-    for device in (at_z(1), at_z(-1), at_y(1), at_y(-1), at_x(1), at_x(-1), sibling):
+    for device in (at_z(1), at_z(-1), at_y(1), at_y(-1), at_y(2), at_x(1), at_x(-1), at_x(2), sibling):
         pl.semaphore_signal(barrier, inc=1, device_id=device, device_id_type=MESH_ID)
 
     s_all[pl.ds(OWN * NR, NR), :] = unit(audio_ref[...])[0].astype(BF16)
@@ -195,61 +201,61 @@
     row_c = c ^ core
     ids[...] = zh * 4096 + row_y * 1024 + row_x * 256 + zl * 128 + row_c * 64 + which * 32 + r
 
-    pl.semaphore_wait(barrier, 7)
-
-    start(("s", L1, 0), ("s", R1, 1), ("t1", 0, 1), ("t1", 0, 2), ("t1", 1, 1), ("t1", 1, 2))
+    pl.semaphore_wait(barrier, 9)
+
+    start(("s", L1, 0), ("s", R1, 1))
+    for slot in (1, 2, 3):
+        start(("t1", 0, slot), ("t1", 1, slot))
     start(("l", L1), ("l", R1), ("s", L1, 1), ("s", R1, 0))
     for w in (0, 1):
         start(("t2", w, 1, 0), ("t2", w, 2, 0))
     t_back[...] = jnp.zeros_like(t_back)
     s_back[...] = jnp.zeros_like(s_back)
-    for w in (0, 1):
-        wait(("t1", w, 1))
-        start(("t1", w, 3, 0), ("t2", w, 1, 1), ("t2", w, 2, 1))
-        wait(("t1", w, 2))
-        start(("t1", w, 3, 1), ("t2", w, 1, 2), ("t2", w, 2, 2))
+    for j in (1, 2):
+        for w in (0, 1):
+            wait(("t1", w, j))
+            start(("t2", w, 1, j), ("t2", w, 2, j))
     wait(("s", L1, 0), ("s", R1, 1))
     start(("s", L2, 0), ("s", R2, 1))
+    for w in (0, 1):
+        wait(("t1", w, 3))
+        start(("t2", w, 1, 3), ("t2", w, 2, 3), ("ts", w, 0))
+    for w in (0, 1):
+        start(*(("t2", w, 3, j) for j in range(4)))
     wait(("l", L1), ("l", R1))
     start(("l", L2), ("l", R2))
-    for w in (0, 1):
-        wait(("t1", w, 3, 0), ("t1", w, 3, 1))
-        start(("t2", w, 1, 3), ("t2", w, 2, 3), ("ts", w, 0))
-    for w in (0, 1):
-        wait(("t2", w, 1, 0), ("t2", w, 1, 1))
-        start(("t2", w, 3, 0))
     wait(("s", L1, 1), ("s", R1, 0))
     start(("s", L2, 1), ("s", R2, 0))
     wait(("ts", 0, 0), ("ts", 1, 0))
 
     def before_0():
-        for w in (0, 1):
-            wait(("t2", w, 2, 2), ("t2", w, 2, 3))
-            start(("t2", w, 3, 1))
-        for w in (0, 1):
-            wait(("t2", w, 1, 2), ("t2", w, 1, 3))
-            start(("ts", w, 1))
-            wait(("t2", w, 2, 0), ("t2", w, 2, 1))
-            start(("ts", w, 2))
+        for slot in (1, 2):
+            for w in (0, 1):
+                wait(*(("t2", w, slot, j) for j in range(4)))
+                start(("ts", w, slot))
         wait(("s", L2, 0), ("s", R2, 1), ("l", L2), ("l", R2))
         start(("s", L3, 0), ("s", R3, 1), ("l", L3), ("l", R3))
         wait(("ts", 0, 1), ("ts", 1, 1))
 
     def before_1():
         wait(("ts", 0, 2), ("ts", 1, 2))
-        for w in (0, 1):
-            wait(("t2", w, 3, 0), ("t2", w, 3, 1))
-            start(("ts", w, 3))
 
     def before_2():
         wait(("s", L2, 1), ("s", R2, 0))
         start(("s", L3, 1), ("s", R3, 0))
-        wait(("ts", 0, 3), ("ts", 1, 3))
+
+    def before_3():
+        for w in (0, 1):
+            wait(*(("t2", w, 3, j) for j in range(4)))
+            start(("ts", w, 3))
 
     def before_4():
         wait(("s", L3, 0), ("s", R3, 1), ("l", L3), ("l", R3))
         start(("s", D4, 0), ("s", D4, 1), ("l", D4))
 
+    def before_5():
+        wait(("ts", 0, 3), ("ts", 1, 3))
+
     def before_7():
         wait(("s", L3, 1), ("s", R3, 0))
 
@@ -264,7 +270,7 @@
         start(("sr", 3))
 
     before = {
-        0: before_0, 1: before_1, 2: before_2, 4: before_4, 7: before_7, 11: before_11,
+        0: before_0, 1: before_1, 2: before_2, 3: before_3, 4: before_4, 5: before_5, 7: before_7, 11: before_11,
         12: before_12, 13: before_13,
     }
 
@@ -272,9 +278,10 @@
     shift = shift_ref[0]
 
     def place(i):
-        u = i // 4
         n = i % 4
-        k = jnp.where(u == 3, jnp.where(n == 0, 3, jnp.where(n == 3, 0, n)), n)
+        u = jnp.where(i < 6, i // 3, jnp.where(i < 8, i - 6, i // 4))
+        k = jnp.where(i < 6, i % 3, jnp.where(i < 8, 3, n))
+        k = jnp.where(i < 12, k, jnp.where(n == 0, 3, jnp.where(n == 3, 0, n)))
         return pl.multiple_of(u * 256, 256), pl.multiple_of(k * CHUNK, CHUNK), pl.multiple_of(u * 16, 16)
 
     def forward(i, coefs):
@@ -322,64 +329,54 @@
         wait(("sr", k))
         add(t_back.at[pl.ds(t_base(k, 0, 0), 2 * SLAB)], sib_back.at[pl.ds(k * 2 * SLAB, 2 * SLAB)])
 
-    def z_step(order, pieces):
-        for p in pieces:
-            for step, chain in chains.items():
-                piece = p if step == 1 else (p + 2) % 4
-                ref = sb(chain[order + 1], piece)
-                ref[...] += landed(("zr", step, order, piece))
-                if order < 3:
-                    ship(("zr", step, order + 1, piece))
+    def z_step(order, *pieces):
+        both = [(step, p if step == 1 else (p + 2) % 4) for p in pieces for step in (1, -1)]
+        if order < 3:
+            forward_sum(*((("zr", step, order, p), ("zr", step, order + 1, p)) for step, p in both))
+            return
+        for step, p in both:
+            arrived(("zr", step, order, p))
+            ref = sb(OWN, p)
+            ref[...] += unpacked(("zr", step, order, p))
+
+    def ship_slabs(k):
+        merge_sibling(k)
+        ship(*(("r2", w, k, half) for w in (0, 1) for half in (0, 1)))
 
     start(("sr", 1))
     forward(15, coef_odd)
     backward(14, coef_even)
     start(("sr", 2))
-    merge_sibling(3)
-    for w in (0, 1):
-        ship(("r2", w, 1, 0, 0), ("r2", w, -1, 0, 1))
     backward(15, coef_odd)
+    ship(("zr", 1, 0, 0), ("zr", -1, 0, 2))
     start(("sr", 0))
-    ship(("zr", 1, 0, 0), ("zr", -1, 0, 2), ("zr", 1, 0, 1), ("zr", -1, 0, 3))
-    merge_sibling(1)
-    for w in (0, 1):
-        ship(("r2", w, -1, 1, 0))
-    merge_sibling(2)
-    for w in (0, 1):
-        ship(("r2", w, 1, 1, 1))
-    z_step(1, (2, 3))
-    z_step(0, (0, 1))
-    for w in (0, 1):
-        ref = tb(2, w, 0, 64)
-        ref[...] += landed(("r2", w, 1, 0, 0))
-        ship(("r2", w, 1, 1, 0))
-        ref = tb(1, w, 64, 64)
-        ref[...] += landed(("r2", w, -1, 0, 1))
-        ship(("r2", w, -1, 1, 1))
+    ship(("zr", 1, 0, 1), ("zr", -1, 0, 3))
+    ship_slabs(3)
+    z_step(1, 2, 3)
+    ship_slabs(1)
+    ship_slabs(2)
+    z_step(0, 0)
+    z_step(0, 1)
     merge_sibling(0)
-    z_step(2, (2, 3))
-    z_step(1, (0, 1))
-    for w in (0, 1):
-        for half, step in ((1, 1), (0, -1), (0, 1), (1, -1)):
-            ref = tb(0, w, half * 64, 64)
-            ref[...] += landed(("r2", w, step, 1, half))
-        ship(("r1", w, 1, 0, 0), ("r1", w, -1, 0, 1), ("r1", w, 1, 1, 1), ("r1", w, -1, 1, 0))
-    z_step(2, (0, 1))
-    for w in (0, 1):
-        ref = tb(0, w, 2 * SUB, 16)
-        ref[...] += landed(("r1", w, 1, 0, 0))
-        ship(("r1", w, 1, 1, 0))
-        ref = tb(0, w, SUB + 16, 16)
-        ref[...] += landed(("r1", w, -1, 0, 1))
-        ship(("r1", w, -1, 1, 1))
-    z_step(3, (2, 3))
+    z_step(2, 2, 3)
+    z_step(1, 0)
+    z_step(1, 1)
     for w in (0, 1):
         for half in (0, 1):
-            ref = tb(0, w, half * 16, 16)
-            ref[...] += landed(("r1", w, 1, 1, half)) + landed(("r1", w, -1, 1, half))
+            for slot in (3, 1, 2):
+                arrived(("r2", w, slot, half))
+            ref = tb(0, w, half * 64, 64)
+            ref[...] += unpacked(("r2", w, 3, half)) + unpacked(("r2", w, 1, half)) + unpacked(("r2", w, 2, half))
+        ship(*(("r1", w, slot) for slot in (3, 2, 1)))
+    z_step(3, 2, 3)
+    z_step(2, 0)
+    z_step(2, 1)
+    for w in (0, 1):
+        arrived(*(("r1", w, slot) for slot in (1, 2, 3)))
+        back = tb(0, w, 0, SUB)[...] + unpacked(("r1", w, 1)) + unpacked(("r1", w, 2)) + unpacked(("r1", w, 3))
         rows = pl.ds(w * SUB, SUB)
-        text_out[rows, :] = project(tb(0, w, 0, SUB)[...], text_ref[rows, :])
-    z_step(3, (0, 1))
+        text_out[rows, :] = project(back, text_ref[rows, :])
+    z_step(3, 0, 1)
     speech_out[...] = project(s_back[pl.ds(OWN * NR, NR), :], audio_ref[...])
 
     for done in copies.values():
@@ -387,9 +384,9 @@
     assert len(copies) == COPIES and len(routes) == ROUTES and used[0] == Q_ROWS
 
 
-ROUTES = 28 + 12 + 12
-Q_ROWS = 28 * PIECE + 12 * 64 + 12 * 16
-COPIES = 14 + 7 + 2 * (4 + 8 + 2 + 4) + 4 + 2 * ROUTES
+ROUTES = 28 + 12 + 6
+Q_ROWS = 28 * PIECE + 12 * 64 + 6 * SUB
+COPIES = 14 + 7 + 2 * (3 + 12 + 4) + 4 + 2 * ROUTES
 
 
 def shards(audio, sentence, matching, sharpness, offset):

time: 70.1 us -> 65.6 us (0.936)
  Pallas kernels: 65.5 us -> 61 us
    pallas_call x1, Pallas kernels: 65.5 us -> 61 us  [shards(): pl.pallas_call(kernel, out_shape=(jax.ShapeDtypeStruct((NR, E), F32), jax...]
where the time goes in v4:
time: 65.6 us; the launch traced here: 65.4 us
  Pallas kernels  61 us (93%)
  local copies, waits for them, and re-layouts  2.49 us (4%)
  between operations  1.94 us (3%)
    pallas_call x1, Pallas kernels, shards(): pl.pallas_call(kernel, out_shape=(jax.ShapeDtypeStruct((NR, E), F32), jax...  61 us
    unnamed x4, local copies, waits for them, and re-layouts  2.49 us

profile of v4, /device:TPU:1, one launch (start us, length us, event | category | flops | bytes accessed | tf_op | source)
XLA Modules:
  0.0 65.4 jit_solution(2699564044968791050)
XLA Ops:
  1.9 61.0 %shard_map.68 = (f32[128,768]{1,0:T(8,128)}, f32[64,768]{1,0:T(8,128)}) custom-call(f32[1]{0:T(128)S(6)} %copy.9.sharp_ref, f32[1]{0:T(128)S(6)} %copy.10.shift_ref, bf16[128,768]{1,0:T(8,128)(2,1)} %audio_ref.1, bf16[64,768]{1,0:T(8,128)(2,1)} %text_ref.1, s32[1,128]{1,0:T(1,128)} %bitcast.1), custom_call_target="tpu_custom_call" | custom-call | tf_op jit(solution)/shard_map/pallas_call | solution.py:395
  62.9 0.0 copy-start
  62.9 1.8 %copy.11 = f32[128,768]{1,0:T(8,128)} copy(f32[128,768]{1,0:T(8,128)} %get-tuple-element.4) | data formatting | bytes 786432
  64.8 0.0 copy-done
  64.8 0.7 %copy.12 = f32[64,768]{1,0:T(8,128)} copy(f32[64,768]{1,0:T(8,128)S(1)} %copy-done) | data formatting | bytes 393216
Async XLA Ops:
  62.9 1.8 %copy-start = (f32[64,768]{1,0:T(8,128)S(1)}, f32[64,768]{1,0:T(8,128)}, u32[]{:S(2)}) copy-start(f32[64,768]{1,0:T(8,128)} %get-tuple-element.5) | copy-start | bytes 589828

commit v5 on v4

--- a/solution.py
+++ b/solution.py
@@ -101,8 +101,9 @@
         piece = lambda j, lo=0, n=SUB: t_rows(0, 0, w, j * SUB + lo, n)
         for slot, step in ((1, 1), (2, -1), (3, 2)):
             copy(("t1", w, slot), piece(0), piece(slot), first(step))
-            for j in range(4):
+            for j in range(4 if slot < 3 else 2):
                 copy(("t2", w, slot, j), piece(j), t_rows(slot, 0, w, j * SUB, SUB), second(step))
+        copy(("t2", w, 3, 2), t_rows(2, 0, w, 64, 64), t_rows(3, 0, w, 64, 64), second(-1))
         for k in range(4):
             copy(("ts", w, k), t_rows(k, 0, w, 0, SLAB), t_rows(k, 1, w, 0, SLAB), sibling)
 
@@ -163,7 +164,8 @@
         for order, src in enumerate(chain[:-1]):
             for piece in range(4):
                 if src != D4 or piece in far_pieces[step]:
-                    route(("zr", step, order, piece), sb(src, piece), PIECE, at_z(step))
+                    to = at_z(2 * step if src == D4 else step)
+                    route(("zr", step, order, piece), sb(src, piece), PIECE, to)
 
     def tb(k, which, first, count):
         return t_back.at[pl.ds(t_base(k, 0, which) + first, count)]
@@ -176,11 +178,12 @@
     for w, (first, second) in enumerate(((at_x, at_y), (at_y, at_x))):
         for slot, step in ((3, 2), (2, 1), (1, -1)):
             for half in (0, 1):
-                route(("r2", w, slot, half), tb(slot, w, half * 64, 64), 64, second(step))
+                to = second(-1 if slot == 3 and half == 1 else step)
+                route(("r2", w, slot, half), tb(slot, w, half * 64, 64), 64, to)
             route(("r1", w, slot), tb(0, w, slot * SUB, SUB), SUB, first(step))
 
     barrier = pltpu.get_barrier_semaphore()
-    for device in (at_z(1), at_z(-1), at_y(1), at_y(-1), at_y(2), at_x(1), at_x(-1), at_x(2), sibling):
+    for device in (at_z(1), at_z(-1), at_z(2), at_z(-2), at_y(1), at_y(-1), at_y(2), at_x(1), at_x(-1), at_x(2), sibling):
         pl.semaphore_signal(barrier, inc=1, device_id=device, device_id_type=MESH_ID)
 
     s_all[pl.ds(OWN * NR, NR), :] = unit(audio_ref[...])[0].astype(BF16)
@@ -201,7 +204,7 @@
     row_c = c ^ core
     ids[...] = zh * 4096 + row_y * 1024 + row_x * 256 + zl * 128 + row_c * 64 + which * 32 + r
 
-    pl.semaphore_wait(barrier, 9)
+    pl.semaphore_wait(barrier, 11)
 
     start(("s", L1, 0), ("s", R1, 1))
     for slot in (1, 2, 3):
@@ -221,7 +224,7 @@
         wait(("t1", w, 3))
         start(("t2", w, 1, 3), ("t2", w, 2, 3), ("ts", w, 0))
     for w in (0, 1):
-        start(*(("t2", w, 3, j) for j in range(4)))
+        start(("t2", w, 3, 0), ("t2", w, 3, 1))
     wait(("l", L1), ("l", R1))
     start(("l", L2), ("l", R2))
     wait(("s", L1, 1), ("s", R1, 0))
@@ -229,9 +232,12 @@
     wait(("ts", 0, 0), ("ts", 1, 0))
 
     def before_0():
+        for w in (0, 1):
+            wait(("t2", w, 2, 2), ("t2", w, 2, 3))
+            start(("t2", w, 3, 2))
         for slot in (1, 2):
             for w in (0, 1):
-                wait(*(("t2", w, slot, j) for j in range(4)))
+                wait(*(("t2", w, slot, j) for j in range(4 if slot == 1 else 2)))
                 start(("ts", w, slot))
         wait(("s", L2, 0), ("s", R2, 1), ("l", L2), ("l", R2))
         start(("s", L3, 0), ("s", R3, 1), ("l", L3), ("l", R3))
@@ -246,7 +252,7 @@
 
     def before_3():
         for w in (0, 1):
-            wait(*(("t2", w, 3, j) for j in range(4)))
+            wait(*(("t2", w, 3, j) for j in range(3)))
             start(("ts", w, 3))
 
     def before_4():
@@ -263,8 +269,8 @@
         wait(("s", D4, 0), ("s", D4, 1), ("l", D4))
 
     def before_12():
-        for step, pieces in ((1, (2, 3)), (-1, (0, 1))):
-            ship(*(("zr", step, 1, piece) for piece in pieces))
+        for pieces in ((2, 3), (0, 1)):
+            ship(*(("zr", step, 1, p if step == 1 else (p + 2) % 4) for p in pieces for step in (1, -1)))
 
     def before_13():
         start(("sr", 3))
@@ -339,45 +345,53 @@
             ref = sb(OWN, p)
             ref[...] += unpacked(("zr", step, order, p))
 
-    def ship_slabs(k):
+    def z_far(piece):
+        both = [(step, piece if step == 1 else (piece + 2) % 4) for step in (1, -1)]
+        for step, p in both:
+            arrived(("zr", step, 0, p), ("zr", step, 1, p))
+        for step, p in both:
+            leave = ("zr", step, 2, p)
+            pack(leave, routes[leave][0][...] + unpacked(("zr", step, 1, p)) + unpacked(("zr", step, 0, p)))
+        send(*(("zr", step, 2, p) for step, p in both))
+
+    def ship_slabs(k, halves):
         merge_sibling(k)
-        ship(*(("r2", w, k, half) for w in (0, 1) for half in (0, 1)))
+        ship(*(("r2", w, k, half) for w in (0, 1) for half in halves))
 
     start(("sr", 1))
     forward(15, coef_odd)
     backward(14, coef_even)
     start(("sr", 2))
     backward(15, coef_odd)
+    start(("sr", 0))
     ship(("zr", 1, 0, 0), ("zr", -1, 0, 2))
-    start(("sr", 0))
     ship(("zr", 1, 0, 1), ("zr", -1, 0, 3))
-    ship_slabs(3)
+    ship_slabs(3, (1, 0))
     z_step(1, 2, 3)
-    ship_slabs(1)
-    ship_slabs(2)
-    z_step(0, 0)
-    z_step(0, 1)
+    ship_slabs(1, (0,))
+    ship_slabs(2, (0, 1))
+    z_far(0)
+    z_far(1)
+    forward_sum(*((("r2", w, 3, 1), ("r2", w, 1, 1)) for w in (0, 1)))
+    z_step(2, 2, 3)
     merge_sibling(0)
-    z_step(2, 2, 3)
-    z_step(1, 0)
-    z_step(1, 1)
+    z_step(2, 0)
+    z_step(2, 1)
+    for half, slots in ((0, (1, 3, 2)), (1, (2, 1))):
+        for w in (0, 1):
+            arrived(*(("r2", w, slot, half) for slot in slots))
+            ref = tb(0, w, half * 64, 64)
+            ref[...] += sum(unpacked(("r2", w, slot, half)) for slot in slots)
     for w in (0, 1):
-        for half in (0, 1):
-            for slot in (3, 1, 2):
-                arrived(("r2", w, slot, half))
-            ref = tb(0, w, half * 64, 64)
-            ref[...] += unpacked(("r2", w, 3, half)) + unpacked(("r2", w, 1, half)) + unpacked(("r2", w, 2, half))
         ship(*(("r1", w, slot) for slot in (3, 2, 1)))
     z_step(3, 2, 3)
-    z_step(2, 0)
-    z_step(2, 1)
+    z_step(3, 0, 1)
+    speech_out[...] = project(s_back[pl.ds(OWN * NR, NR), :], audio_ref[...])
     for w in (0, 1):
         arrived(*(("r1", w, slot) for slot in (1, 2, 3)))
         back = tb(0, w, 0, SUB)[...] + unpacked(("r1", w, 1)) + unpacked(("r1", w, 2)) + unpacked(("r1", w, 3))
         rows = pl.ds(w * SUB, SUB)
         text_out[rows, :] = project(back, text_ref[rows, :])
-    z_step(3, 0, 1)
-    speech_out[...] = project(s_back[pl.ds(OWN * NR, NR), :], audio_ref[...])
 
     for done in copies.values():
         done.wait_send()
@@ -386,7 +400,7 @@
 
 ROUTES = 28 + 12 + 6
 Q_ROWS = 28 * PIECE + 12 * 64 + 6 * SUB
-COPIES = 14 + 7 + 2 * (3 + 12 + 4) + 4 + 2 * ROUTES
+COPIES = 14 + 7 + 2 * (3 + 11 + 4) + 4 + 2 * ROUTES
 
 
 def shards(audio, sentence, matching, sharpness, offset):

time: 65.6 us -> 65 us (level)
  Pallas kernels: 61 us -> 60.1 us
    pallas_call x1, Pallas kernels: 61 us -> 60.1 us  [shards(): pl.pallas_call(kernel, out_shape=(jax.ShapeDtypeStruct((NR, E), F32), jax...]
where the time goes in v5:
time: 65 us; the launch traced here: 64.6 us
  Pallas kernels  60.1 us (92%)
  local copies, waits for them, and re-layouts  2.49 us (4%)
  between operations  1.94 us (3%)
    pallas_call x1, Pallas kernels, shards(): pl.pallas_call(kernel, out_shape=(jax.ShapeDtypeStruct((NR, E), F32), jax...  60.1 us
    unnamed x4, local copies, waits for them, and re-layouts  2.49 us

profile of v5, /device:TPU:1, one launch (start us, length us, event | category | flops | bytes accessed | tf_op | source)
XLA Modules:
  0.0 64.6 jit_solution(634974387453802695)
XLA Ops:
  1.9 60.1 %shard_map.68 = (f32[128,768]{1,0:T(8,128)}, f32[64,768]{1,0:T(8,128)}) custom-call(f32[1]{0:T(128)S(6)} %copy.9.sharp_ref, f32[1]{0:T(128)S(6)} %copy.10.shift_ref, bf16[128,768]{1,0:T(8,128)(2,1)} %audio_ref.1, bf16[64,768]{1,0:T(8,128)(2,1)} %text_ref.1, s32[1,128]{1,0:T(1,128)} %bitcast.1), custom_call_target="tpu_custom_call" | custom-call | tf_op jit(solution)/shard_map/pallas_call | solution.py:409
  62.1 0.0 copy-start
  62.1 1.8 %copy.11 = f32[128,768]{1,0:T(8,128)} copy(f32[128,768]{1,0:T(8,128)} %get-tuple-element.4) | data formatting | bytes 786432
  63.9 0.0 copy-done
  63.9 0.7 %copy.12 = f32[64,768]{1,0:T(8,128)} copy(f32[64,768]{1,0:T(8,128)S(1)} %copy-done) | data formatting | bytes 393216
Async XLA Ops:
  62.1 1.8 %copy-start = (f32[64,768]{1,0:T(8,128)S(1)}, f32[64,768]{1,0:T(8,128)}, u32[]{:S(2)}) copy-start(f32[64,768]{1,0:T(8,128)} %get-tuple-element.5) | copy-start | bytes 589828
